TPU v7x, 32 devices: a whole 2x2x4 slice. The times are simulated.
32 devices in a mesh: grp: 2 (over x), row: 4 (over y, core), col: 4 (over z).
Axes of the slice: x: 2, y: 2, z: 4, core: 2. Of those that a mesh axis runs over, the one named last changes fastest.
Arguments:
- gradients: bfloat16 [2, 3072, 24576], P('grp', 'row', 'col'), may hold values from -6 to 6
- momentum: float32 [2, 3072, 24576], P('grp', 'row', 'col'), may hold values from -94 to 94, as said below
- right_basis: bfloat16 [24576, 512], P('col'), may hold values from -6 to 6
Outputs:
- new_momentum: float32 [2, 3072, 24576], P('grp', 'row', 'col')
- new_basis: bfloat16 [24576, 512], P('col')
- update: bfloat16 [3072, 24576], P('row', 'col')
Inputs may be any that keep to these rules, and one draw needn't show every extreme that they name: Each group's momentum buffer holds real values bounded in magnitude by 94.
All inputs are finite; a program needn't handle non-finite values.
Results may differ from a plain program's by a relative error of at most 0.013.
Values may be sent and summed in bfloat16 or wider, within the bound.
No kernel may reach another device: no remote copies, remote signals or barrier semaphores. Data moves between devices by JAX's collectives and lax.ppermute only.
A program may use at most 192 MiB of HBM per device.

v0:
```python
import math
import jax
import jax.numpy as jnp
from jax import lax
from jax.sharding import PartitionSpec as P

D = 3072
FF = 24576
momentum_decay = 0.9
ridge_scale = 0.0001
epsilon = 1e-06


def per_device(gradients, momentum, right_basis):
    merged = momentum[0] + gradients[0].astype(jnp.float32)
    merged_low = merged.astype(jnp.bfloat16)
    rank = right_basis.shape[1]
    local_rows = merged.shape[0]
    groups = lax.axis_size("grp")
    left_factor = jnp.dot(merged_low, right_basis, preferred_element_type=jnp.float32)
    left_factor = lax.psum(left_factor, ("grp", "col"))
    gram_matrix = jnp.dot(
        left_factor.T,
        left_factor,
        precision=lax.Precision.HIGHEST,
        preferred_element_type=jnp.float32,
    )
    gram_matrix = lax.psum(gram_matrix, "row")
    shifted = gram_matrix + ridge_scale * (jnp.trace(gram_matrix) / rank) * jnp.eye(
        rank, dtype=jnp.float32
    )
    cholesky_factor = jnp.linalg.cholesky(shifted)
    orthonormal = jax.scipy.linalg.solve_triangular(cholesky_factor, left_factor.T, lower=True).T
    orthonormal_low = orthonormal.astype(jnp.bfloat16)
    right_piece = lax.psum_scatter(
        jnp.einsum("ij,ik->jk", merged_low, orthonormal_low, preferred_element_type=jnp.float32)
        / groups,
        ("grp", "row"),
        scatter_dimension=0,
        tiled=True,
    )
    squares_sum = lax.psum(jnp.sum(right_piece * right_piece, axis=0), ("grp", "row", "col"))
    column_rms = jnp.sqrt(squares_sum / FF + epsilon)
    basis_piece = (right_piece / column_rms).astype(jnp.bfloat16)
    new_basis = lax.all_gather(basis_piece, ("grp", "row"), axis=0, tiled=True)
    scaled_low = (orthonormal * column_rms).astype(jnp.bfloat16)
    stacked_left = jnp.concatenate([orthonormal_low, scaled_low], axis=0)
    products = lax.dot_general(
        stacked_left, new_basis, (((1,), (1,)), ((), ())), preferred_element_type=jnp.float32
    )
    update = (math.sqrt(D / rank) * products[:local_rows]).astype(jnp.bfloat16)
    new_momentum = merged - (1 - momentum_decay) * products[local_rows:]
    return (new_momentum[None], new_basis, update)


def solution(mesh):
    placed = (P("grp", "row", "col"), P("grp", "row", "col"), P("col", None))
    return jax.shard_map(
        per_device,
        mesh=mesh,
        in_specs=placed,
        out_specs=(P("grp", "row", "col"), P("col", None), P("row", "col")),
        check_vma=False,
    )
```

profile of v0, /device:TPU:0, one launch (start us, length us, event | category | flops | bytes accessed | tf_op | source)
XLA Modules:
  0.0 571.5 jit_solution(11298034672186041902)
XLA Ops:
  7.2 14.6 %fusion.42 = f32[768,512]{1,0:T(8,128)} fusion(bf16[6144,512]{1,0:T(8,128)(2,1)} %param.5, f32[1,768,6144]{2,1,0:T(8,128)} %param.4, bf16[1,768,6144]{2,1,0:T(8,128)(2,1)} %param.3), kind=kOutput, calls=%fused_computation.89 | convolution fusion | flops 4845993984 | bytes 36175872 | tf_op jit(solution)/shard_map/dot_general | solution.py:20
  21.9 92.1 %all-reduce.4.cloned.1.call-done = f32[768,512]{1,0:T(8,128)} async-done(((f32[768,512]{1,0:T(8,128)}), f32[768,512]{1,0:T(8,128)}) %all-reduce.4.cloned.1.call-update) | async-done | bytes 1572880 | tf_op jit(solution)/shard_map/psum | solution.py:21
  114.0 5.6 fusion.44
  119.9 35.5 %all-reduce.6.cloned.1.call-done = f32[512,512]{0,1:T(8,128)} async-done(((f32[512,512]{0,1:T(8,128)}), f32[512,512]{0,1:T(8,128)}) %all-reduce.6.cloned.1.call-update) | async-done | bytes 1048592 | tf_op jit(solution)/shard_map/psum | solution.py:28
  155.3 2.0 select_reduce_fusion
  158.7 11.7 %cholesky.103 = f32[128,128]{1,0:T(8,128)S(1)} custom-call(f32[128,128]{1,0:T(8,128)S(1)} %cholesky.263), custom_call_target="Cholesky" | custom-call | tf_op jit(solution)/shard_map/jit(cholesky)/cholesky | solution.py:32
  170.6 9.8 %custom-call.31 = f32[1,128,128]{1,2,0:T(8,128)S(1)} custom-call(f32[1,128,128]{2,1,0:T(8,128)S(1)} %get-tuple-element.32), custom_call_target="InvertDiagBlocksLowerTriangular" | custom-call | tf_op jit(solution)/shard_map/jit(cholesky)/cholesky | solution.py:32
  181.2 11.7 %cholesky.215 = f32[128,128]{1,0:T(8,128)S(1)} custom-call(f32[128,128]{1,0:T(8,128)S(1)} %cholesky.267), custom_call_target="Cholesky" | custom-call | tf_op jit(solution)/shard_map/jit(cholesky)/cholesky | solution.py:32
  193.0 10.0 %custom-call.32 = f32[1,128,128]{1,2,0:T(8,128)S(1)} custom-call(f32[1,128,128]{2,1,0:T(8,128)S(1)} %get-tuple-element.30), custom_call_target="InvertDiagBlocksLowerTriangular" | custom-call | tf_op jit(solution)/shard_map/jit(cholesky)/cholesky | solution.py:32
  203.5 0.6 convolution_subtract_fusion.4
  204.1 11.7 %cholesky.236 = f32[128,128]{1,0:T(8,128)S(1)} custom-call(f32[128,128]{1,0:T(8,128)S(1)} %cholesky.272), custom_call_target="Cholesky" | custom-call | tf_op jit(solution)/shard_map/jit(cholesky)/cholesky | solution.py:32
  216.0 9.8 %custom-call.33 = f32[1,128,128]{1,2,0:T(8,128)S(1)} custom-call(f32[1,128,128]{2,1,0:T(8,128)S(1)} %get-tuple-element.28), custom_call_target="InvertDiagBlocksLowerTriangular" | custom-call | tf_op jit(solution)/shard_map/jit(cholesky)/cholesky | solution.py:32
  226.6 12.1 %cholesky.253 = f32[128,128]{1,0:T(8,128)S(1)} custom-call(f32[128,128]{1,0:T(8,128)S(1)} %convolution_subtract_fusion.5), custom_call_target="Cholesky" | custom-call | tf_op jit(solution)/shard_map/jit(cholesky)/cholesky | solution.py:32
  238.8 0.7 compare_reduce_fusion.1
  239.5 0.7 compare_reduce_fusion
  240.2 0.7 compare_reduce_fusion.2
  243.4 1.1 select_select_fusion
  244.5 14.5 %while.1 = (s32[]{:T(128)}, f32[512,512]{0,1:T(8,128)}, s32[4,2]{0,1:T(2,128)S(1)}, f32[4,128,128]{2,1,0:T(8,128)}, s32[]{:T(128)}) while((s32[]{:T(128)}, f32[512,512]{0,1:T(8,128)}, s32[4,2]{0,1:T(2,128)S(1)}, f32[4,128,128]{2,1,0:T(8,128)}, s32[]{:T(128)}) %tuple.29), condition=%wide.while_cond, body=%wide.while_body.sunk | while | flops 2 | bytes 393329 | solution.py:33
  244.6 0.6 fusion.55
  245.2 2.2 dynamic-slice.7
  247.5 0.6 bitcast_dynamic-update-slice_fusion.2
  248.2 0.6 fusion.55
  248.8 2.2 dynamic-slice.7
  251.2 0.6 bitcast_dynamic-update-slice_fusion.2
  251.9 0.6 fusion.55
  252.5 2.2 dynamic-slice.7
  254.8 0.6 bitcast_dynamic-update-slice_fusion.2
  255.5 0.6 fusion.55
  256.1 2.2 dynamic-slice.7
  258.4 0.6 bitcast_dynamic-update-slice_fusion.2
  259.0 40.1 %custom-call.34 = f32[4,128,128]{1,2,0:T(8,128)S(1)} custom-call(f32[4,128,128]{2,1,0:T(8,128)} %get-tuple-element.10), custom_call_target="InvertDiagBlocksLowerTriangular" | custom-call | tf_op jit(solution)/shard_map/jit(_solve_triangular)/triangular_solve | solution.py:33
  299.1 0.5 fusion.18
  299.7 1.6 convolution_subtract_fusion.1
  301.3 0.5 fusion.31
  301.8 2.3 convolution_subtract_fusion.2
  304.2 0.5 fusion.29
  304.7 3.0 convolution_subtract_fusion
  307.7 0.5 fusion.28
  308.2 19.8 %convolution_multiply_fusion = f32[6144,512]{1,0:T(8,128)} fusion(f32[128,768]{1,0:T(8,128)S(1)} %fusion.28, f32[128,768]{1,0:T(8,128)S(1)} %fusion.29, f32[128,768]{1,0:T(8,128)S(1)} %fusion.31, f32[128,768]{1,0:T(8,128)S(1)} %fusion.18, f32[1,768,6144]{2,1,0:T(8,128)} %param.4, bf16[1,768,6144]{2,1,0:T(8,128)(2,1)} %param.3), kind=kOutput, calls=%fused_computation.9 | convolution fusion | flops 4852285440 | bytes 42467328 | tf_op jit(solution)/shard_map/ij,ik->jk/dot_general | solution.py:36
  328.1 92.8 %reduce-scatter.2.cloned.1.call-done = f32[768,512]{1,0:T(8,128)} async-done(((f32[6144,512]{1,0:T(8,128)}), f32[768,512]{1,0:T(8,128)}) %reduce-scatter.2.cloned.1.call-update) | async-done | bytes 1572880 | tf_op jit(solution)/shard_map/reduce_scatter | solution.py:35
  420.9 1.6 multiply_reduce_fusion
  422.5 39.3 %psum.23 = f32[512]{0:T(512)S(1)} all-reduce(f32[512]{0:T(512)S(1)} %multiply_reduce_fusion), channel_id=1, replica_groups=mesh['grp'=2,'row'=4,'col'=4] {'grp','row','col'}, use_global_device_ids=true, to_apply=%region_13.14 | all-reduce | flops 512 | bytes 4096 | tf_op jit(solution)/shard_map/psum | solution.py:42
  461.8 2.5 divide_convert_fusion
  464.4 1.0 fusion.14
  465.4 45.2 %all-gather.2.cloned.1.call-done = bf16[6144,512]{1,0:T(8,128)(2,1)} async-done(((bf16[768,512]{1,0:T(8,128)(2,1)}), bf16[6144,512]{1,0:T(8,128)(2,1)}) %all-gather.2.cloned.1.call-update) | async-done | bytes 6291472 | tf_op jit(solution)/shard_map/all_gather | solution.py:45
  510.6 19.5 %fusion.3 = f32[1536,6144]{1,0:T(8,128)} fusion(bf16[6144,512]{1,0:T(8,128)(2,1)} %all-gather.2.cloned.1.call-done, bf16[768,512]{0,1:T(8,128)(2,1)} %fusion.14, bf16[768,512]{0,1:T(8,128)(2,1)S(1)} %fusion.41), kind=kOutput, calls=%fused_computation.11 | convolution fusion | flops 9666822144 | bytes 45613056 | tf_op jit(solution)/shard_map/dot_general | solution.py:48
  530.1 32.0 %fusion = (bf16[768,6144]{1,0:T(8,128)(2,1)}, f32[1,768,6144]{2,1,0:T(8,128)}) fusion(f32[1536,6144]{1,0:T(8,128)} %fusion.3, f32[1,768,6144]{2,1,0:T(8,128)} %param.4, bf16[1,768,6144]{2,1,0:T(8,128)(2,1)} %param.3), kind=kLoop, calls=%fused_computation.3 | loop fusion | flops 28311552 | bytes 94371840 | tf_op jit(solution)/shard_map/convert_element_type | solution.py:51
  562.1 2.7 copy.40
  (55 shorter events, 4.4 us)
Async XLA Ops:
  7.2 106.9 %all-reduce.4.cloned.1.call-start = ((), (), s32[]{:S(2)}) async-start(), calls=%async_computation.1 | async-start | bytes 3145728 | tf_op jit(solution)/shard_map/psum | solution.py:21
  21.9 133.5 %all-reduce.6.cloned.1.call-start = ((), (), s32[]{:S(2)}) async-start(), calls=%async_computation.2 | async-start | bytes 2097152 | tf_op jit(solution)/shard_map/psum | solution.py:28
  119.6 301.3 %reduce-scatter.2.cloned.1.call-start = ((), (), s32[]{:S(2)}) async-start(), calls=%async_computation.3 | async-start | bytes 14155776 | tf_op jit(solution)/shard_map/reduce_scatter | solution.py:35
  155.3 2.6 copy-start.1
  243.4 55.7 %copy-start = (f32[768,512]{1,0:T(8,128)S(1)}, f32[768,512]{1,0:T(8,128)}, u32[]{:S(2)}) copy-start(f32[768,512]{1,0:T(8,128)} %all-reduce.4.cloned.1.call-done) | copy-start | bytes 4718596
  328.0 182.6 %all-gather.2.cloned.1.call-start = ((), (), s32[]{:S(2)}) async-start(), calls=%async_computation.4 | async-start | bytes 7077888 | tf_op jit(solution)/shard_map/all_gather | solution.py:45
  510.6 51.4 %slice-start = ((s8[6291456]{0:T(1024)(128)(4,1)}), s8[2097152]{0:T(1024)(128)(4,1)S(1)}, s32[]{:S(2)}) async-start(s8[6291456]{0:T(1024)(128)(4,1)} %bitcast.66), calls=%async_computation.5 | async-start | bytes 4194304
  530.1 32.0 %slice-start.1 = ((s8[6291456]{0:T(1024)(128)(4,1)}), s8[4194304]{0:T(1024)(128)(4,1)S(1)}, s32[]{:S(2)}) async-start(s8[6291456]{0:T(1024)(128)(4,1)} %bitcast.66), calls=%async_computation.6 | async-start | bytes 8388608
Sparse Core Ops, SparseCore 0:
  22.0 92.0 all-reduce.3
  119.7 35.5 all-reduce.5
  328.2 92.7 reduce-scatter.1
  464.4 46.1 all-gather.1
where the time goes:
time: 576 us; the launch traced here: 571 us
  waiting for transfers between devices  266 us (46%)
  other arithmetic  160 us (28%)
  matrix products  70.8 us (12%)
  blocking collectives  39.3 us (7%)
  local copies, waits for them, and re-layouts  18.2 us (3%)
  between operations  17.4 us (3%)
    reduce_scatter x1, waiting for transfers between devices, per_device(): lax.psum_scatter(jnp.einsum('ij,ik->jk', merged_low, orthonormal_low, pre...  92.8 us
    psum x1, waiting for transfers between devices, per_device(): left_factor = lax.psum(left_factor, ('grp', 'col'))  92.1 us
    another operation x14, other arithmetic, per_device(): cholesky_factor = jnp.linalg.cholesky(shifted)  79 us
    all_gather x1, waiting for transfers between devices, per_device(): new_basis = lax.all_gather(basis_piece, ('grp', 'row'), axis=0, tiled=True)  45.2 us
    another operation x3, other arithmetic, per_device(): jax.scipy.linalg.solve_triangular(cholesky_factor, left_factor.T, lower=T...  41.2 us
    psum x1, blocking collectives, per_device(): lax.psum(jnp.sum(right_piece * right_piece, axis=0), ('grp', 'row', 'col'))  39.3 us
    psum x1, waiting for transfers between devices, per_device(): gram_matrix = lax.psum(gram_matrix, 'row')  35.5 us
    convert_element_type x1, other arithmetic, per_device(): update = (math.sqrt(D / rank) * products[:local_rows]).astype(jnp.bfloat16)  32 us
  transfers between devices with their start and end apart: 4, of which 4 were waited for; matrix products, arithmetic and copies ran while one was open for 0% of the time, Pallas kernels for 0%

commit v1 on v0

--- a/solution.py
+++ b/solution.py
@@ -18,7 +18,8 @@
     local_rows = merged.shape[0]
     groups = lax.axis_size("grp")
     left_factor = jnp.dot(merged_low, right_basis, preferred_element_type=jnp.float32)
-    left_factor = lax.psum(left_factor, ("grp", "col"))
+    plain = lax.all_gather(left_factor, ("grp", "col"))
+    left_factor = jnp.sum(plain, axis=0)
     gram_matrix = jnp.dot(
         left_factor.T,
         left_factor,

time: 576 us -> 675 us (1.17)
  waiting for transfers between devices: 266 us -> 351 us
  other arithmetic: 160 us -> 169 us
    all_gather x0 -> x1, waiting for transfers between devices: none -> 179 us  [per_device(): plain = lax.all_gather(left_factor, ('grp', 'col'))]
    psum x1 -> x0, waiting for transfers between devices: 92.1 us -> none  [per_device(): left_factor = lax.psum(left_factor, ('grp', 'col'))]
where the time goes in v1:
time: 675 us; the launch traced here: 669 us
  waiting for transfers between devices  351 us (52%)
  other arithmetic  169 us (25%)
  matrix products  72.5 us (11%)
  blocking collectives  39.3 us (6%)
  local copies, waits for them, and re-layouts  19.2 us (3%)
  between operations  17.4 us (3%)
    all_gather x1, waiting for transfers between devices, per_device(): plain = lax.all_gather(left_factor, ('grp', 'col'))  179 us
    reduce_scatter x1, waiting for transfers between devices, per_device(): lax.psum_scatter(jnp.einsum('ij,ik->jk', merged_low, orthonormal_low, pre...  92.8 us
    another operation x14, other arithmetic, per_device(): cholesky_factor = jnp.linalg.cholesky(shifted)  79 us
    all_gather x1, waiting for transfers between devices, per_device(): new_basis = lax.all_gather(basis_piece, ('grp', 'row'), axis=0, tiled=True)  45.2 us
    another operation x3, other arithmetic, per_device(): jax.scipy.linalg.solve_triangular(cholesky_factor, left_factor.T, lower=T...  40.4 us
    psum x1, blocking collectives, per_device(): lax.psum(jnp.sum(right_piece * right_piece, axis=0), ('grp', 'row', 'col'))  39.3 us
    psum x1, waiting for transfers between devices, per_device(): gram_matrix = lax.psum(gram_matrix, 'row')  34.4 us
    convert_element_type x1, other arithmetic, per_device(): update = (math.sqrt(D / rank) * products[:local_rows]).astype(jnp.bfloat16)  32 us
  transfers between devices with their start and end apart: 4, of which 4 were waited for; matrix products, arithmetic and copies ran while one was open for 0% of the time, Pallas kernels for 0%

profile of v1, /device:TPU:0, one launch (start us, length us, event | category | flops | bytes accessed | tf_op | source)
XLA Modules:
  0.0 669.0 jit_solution(4554695794556082581)
XLA Ops:
  7.2 14.6 %fusion.42 = f32[768,512]{1,0:T(8,128)} fusion(bf16[6144,512]{1,0:T(8,128)(2,1)} %param.5, f32[1,768,6144]{2,1,0:T(8,128)} %param.4, bf16[1,768,6144]{2,1,0:T(8,128)(2,1)} %param.3), kind=kOutput, calls=%fused_computation.89 | convolution fusion | flops 4845993984 | bytes 36175872 | tf_op jit(solution)/shard_map/dot_general | solution.py:20
  21.9 178.9 %all-gather.6.cloned.1.call-done = f32[6144,512]{1,0:T(8,128)} async-done(((f32[768,512]{1,0:T(8,128)}), f32[6144,512]{1,0:T(8,128)}) %all-gather.6.cloned.1.call-update) | async-done | bytes 12582928 | tf_op jit(solution)/shard_map/all_gather | solution.py:21
  200.8 6.3 reduce_sum.28
  207.2 3.7 fusion.44
  211.1 34.4 %all-reduce.3.cloned.1.call-done = f32[512,512]{0,1:T(8,128)} async-done(((f32[512,512]{0,1:T(8,128)}), f32[512,512]{0,1:T(8,128)}) %all-reduce.3.cloned.1.call-update) | async-done | bytes 1048592 | tf_op jit(solution)/shard_map/psum | solution.py:29
  245.5 2.0 select_reduce_fusion
  248.1 2.3 select_add_fusion
  250.5 2.5 copy.7
  253.0 1.4 fusion.12
  254.5 1.0 copy-done.1
  255.4 11.7 %cholesky.103 = f32[128,128]{1,0:T(8,128)S(1)} custom-call(f32[128,128]{1,0:T(8,128)S(1)} %cholesky.263), custom_call_target="Cholesky" | custom-call | tf_op jit(solution)/shard_map/jit(cholesky)/cholesky | solution.py:33
  267.3 9.8 %custom-call.31 = f32[1,128,128]{1,2,0:T(8,128)S(1)} custom-call(f32[1,128,128]{2,1,0:T(8,128)S(1)} %get-tuple-element.32), custom_call_target="InvertDiagBlocksLowerTriangular" | custom-call | tf_op jit(solution)/shard_map/jit(cholesky)/cholesky | solution.py:33
  277.1 1.2 fusion.23
  278.3 1.3 convolution_subtract_fusion.3
  279.8 11.7 %cholesky.215 = f32[128,128]{1,0:T(8,128)S(1)} custom-call(f32[128,128]{1,0:T(8,128)S(1)} %cholesky.267), custom_call_target="Cholesky" | custom-call | tf_op jit(solution)/shard_map/jit(cholesky)/cholesky | solution.py:33
  291.6 10.0 %custom-call.32 = f32[1,128,128]{1,2,0:T(8,128)S(1)} custom-call(f32[1,128,128]{2,1,0:T(8,128)S(1)} %get-tuple-element.30), custom_call_target="InvertDiagBlocksLowerTriangular" | custom-call | tf_op jit(solution)/shard_map/jit(cholesky)/cholesky | solution.py:33
  302.1 1.5 convolution_subtract_fusion.4
  303.6 11.7 %cholesky.236 = f32[128,128]{1,0:T(8,128)S(1)} custom-call(f32[128,128]{1,0:T(8,128)S(1)} %cholesky.272), custom_call_target="Cholesky" | custom-call | tf_op jit(solution)/shard_map/jit(cholesky)/cholesky | solution.py:33
  315.5 9.8 %custom-call.33 = f32[1,128,128]{1,2,0:T(8,128)S(1)} custom-call(f32[1,128,128]{2,1,0:T(8,128)S(1)} %get-tuple-element.28), custom_call_target="InvertDiagBlocksLowerTriangular" | custom-call | tf_op jit(solution)/shard_map/jit(cholesky)/cholesky | solution.py:33
  325.6 1.3 convolution_subtract_fusion.5
  326.9 12.1 %cholesky.253 = f32[128,128]{1,0:T(8,128)S(1)} custom-call(f32[128,128]{1,0:T(8,128)S(1)} %convolution_subtract_fusion.5), custom_call_target="Cholesky" | custom-call | tf_op jit(solution)/shard_map/jit(cholesky)/cholesky | solution.py:33
  339.2 0.7 compare_reduce_fusion.1
  339.9 0.6 compare_reduce_fusion
  340.5 0.6 compare_reduce_fusion.2
  343.7 1.1 select_select_fusion
  344.8 12.5 %while.1 = (s32[]{:T(128)}, f32[512,512]{0,1:T(8,128)}, s32[4,2]{0,1:T(2,128)S(1)}, f32[4,128,128]{2,1,0:T(8,128)S(1)}, s32[]{:T(128)}) while((s32[]{:T(128)}, f32[512,512]{0,1:T(8,128)}, s32[4,2]{0,1:T(2,128)S(1)}, f32[4,128,128]{2,1,0:T(8,128)S(1)}, s32[]{:T(128)}) %tuple.29), condition=%wide.while_cond, body=%wide.while_body.sunk | while | flops 2 | bytes 393329 | solution.py:34
  344.9 0.6 fusion.55
  345.5 2.3 dynamic-slice.7
  348.0 0.6 fusion.55
  348.6 2.3 dynamic-slice.7
  351.2 0.6 fusion.55
  351.8 2.3 dynamic-slice.7
  354.3 0.6 fusion.55
  354.9 2.3 dynamic-slice.7
  357.3 39.3 %custom-call.34 = f32[4,128,128]{1,2,0:T(8,128)S(1)} custom-call(f32[4,128,128]{2,1,0:T(8,128)S(1)} %get-tuple-element.10), custom_call_target="InvertDiagBlocksLowerTriangular" | custom-call | tf_op jit(solution)/shard_map/jit(_solve_triangular)/triangular_solve | solution.py:34
  397.2 1.6 convolution_subtract_fusion.1
  399.3 2.3 convolution_subtract_fusion.2
  402.2 3.0 convolution_subtract_fusion
  405.7 19.8 %convolution_multiply_fusion = f32[6144,512]{1,0:T(8,128)} fusion(f32[128,768]{1,0:T(8,128)S(1)} %fusion.28, f32[128,768]{1,0:T(8,128)S(1)} %fusion.29, f32[128,768]{1,0:T(8,128)S(1)} %fusion.31, f32[128,768]{1,0:T(8,128)S(1)} %fusion.18, f32[1,768,6144]{2,1,0:T(8,128)} %param.4, bf16[1,768,6144]{2,1,0:T(8,128)(2,1)} %param.3), kind=kOutput, calls=%fused_computation.9 | convolution fusion | flops 4852285440 | bytes 42467328 | tf_op jit(solution)/shard_map/ij,ik->jk/dot_general | solution.py:37
  425.6 92.8 %reduce-scatter.2.cloned.1.call-done = f32[768,512]{1,0:T(8,128)} async-done(((f32[6144,512]{1,0:T(8,128)}), f32[768,512]{1,0:T(8,128)}) %reduce-scatter.2.cloned.1.call-update) | async-done | bytes 1572880 | tf_op jit(solution)/shard_map/reduce_scatter | solution.py:36
  518.4 1.6 multiply_reduce_fusion
  520.0 39.3 %psum.15 = f32[512]{0:T(512)S(1)} all-reduce(f32[512]{0:T(512)S(1)} %multiply_reduce_fusion), channel_id=1, replica_groups=mesh['grp'=2,'row'=4,'col'=4] {'grp','row','col'}, use_global_device_ids=true, to_apply=%region_13.14 | all-reduce | flops 512 | bytes 4096 | tf_op jit(solution)/shard_map/psum | solution.py:43
  559.3 2.5 divide_convert_fusion
  561.9 1.0 fusion.14
  562.9 45.2 %all-gather.4.cloned.1.call-done = bf16[6144,512]{1,0:T(8,128)(2,1)} async-done(((bf16[768,512]{1,0:T(8,128)(2,1)}), bf16[6144,512]{1,0:T(8,128)(2,1)}) %all-gather.4.cloned.1.call-update) | async-done | bytes 6291472 | tf_op jit(solution)/shard_map/all_gather | solution.py:46
  608.1 19.5 %fusion.3 = f32[1536,6144]{1,0:T(8,128)} fusion(bf16[6144,512]{1,0:T(8,128)(2,1)} %all-gather.4.cloned.1.call-done, bf16[768,512]{0,1:T(8,128)(2,1)} %fusion.14, bf16[768,512]{0,1:T(8,128)(2,1)S(1)} %fusion.41), kind=kOutput, calls=%fused_computation.11 | convolution fusion | flops 9666822144 | bytes 45613056 | tf_op jit(solution)/shard_map/dot_general | solution.py:49
  627.6 32.0 %fusion = (bf16[768,6144]{1,0:T(8,128)(2,1)}, f32[1,768,6144]{2,1,0:T(8,128)}) fusion(f32[1536,6144]{1,0:T(8,128)} %fusion.3, f32[1,768,6144]{2,1,0:T(8,128)} %param.4, bf16[1,768,6144]{2,1,0:T(8,128)(2,1)} %param.3), kind=kLoop, calls=%fused_computation.3 | loop fusion | flops 28311552 | bytes 94371840 | tf_op jit(solution)/shard_map/convert_element_type | solution.py:52
  659.6 2.7 copy.39
  (56 shorter events, 4.7 us)
Async XLA Ops:
  7.2 193.7 %all-gather.6.cloned.1.call-start = ((), (), s32[]{:S(2)}) async-start(), calls=%async_computation.4 | async-start | bytes 14155776 | tf_op jit(solution)/shard_map/all_gather | solution.py:21
  21.9 223.7 %all-reduce.3.cloned.1.call-start = ((), (), s32[]{:S(2)}) async-start(), calls=%async_computation.1 | async-start | bytes 2097152 | tf_op jit(solution)/shard_map/psum | solution.py:29
  210.9 307.5 %reduce-scatter.2.cloned.1.call-start = ((), (), s32[]{:S(2)}) async-start(), calls=%async_computation.2 | async-start | bytes 14155776 | tf_op jit(solution)/shard_map/reduce_scatter | solution.py:36
  245.5 7.5 %copy-start = (f32[512,512]{0,1:T(8,128)S(1)}, f32[512,512]{0,1:T(8,128)}, u32[]{:S(2)}) copy-start(f32[512,512]{0,1:T(8,128)} %all-reduce.3.cloned.1.call-done) | copy-start | bytes 3145732
  254.4 1.0 copy-start.1
  425.5 182.6 %all-gather.4.cloned.1.call-start = ((), (), s32[]{:S(2)}) async-start(), calls=%async_computation.3 | async-start | bytes 7077888 | tf_op jit(solution)/shard_map/all_gather | solution.py:46
  608.1 51.4 %slice-start = ((s8[6291456]{0:T(1024)(128)(4,1)}), s8[2097152]{0:T(1024)(128)(4,1)S(1)}, s32[]{:S(2)}) async-start(s8[6291456]{0:T(1024)(128)(4,1)} %bitcast.68), calls=%async_computation.5 | async-start | bytes 4194304
  627.6 32.0 %slice-start.1 = ((s8[6291456]{0:T(1024)(128)(4,1)}), s8[4194304]{0:T(1024)(128)(4,1)S(1)}, s32[]{:S(2)}) async-start(s8[6291456]{0:T(1024)(128)(4,1)} %bitcast.68), calls=%async_computation.6 | async-start | bytes 8388608
Sparse Core Ops, SparseCore 0:
  22.0 178.8 all-gather.5
  211.0 34.4 all-reduce.2
  425.6 92.7 reduce-scatter.1
  561.9 46.1 all-gather.3
